TPU v7x, 1024 devices: a whole 4x8x16 slice. The times are simulated.
1024 devices in a mesh: row: 64 (over y, z_lo, core), col: 16 (over x, z_hi).
Axes of the slice: x: 4, y: 8, z: 16 (z_hi: 4, z_lo: 4; z = z_hi * 4 + z_lo), core: 2. Of those that a mesh axis runs over, the one named last changes fastest.
Arguments:
- left_panels: float32 [3, 512, 65536], P(None, 'col', 'row'), may hold values from -0.0234375 to 0.0234375
- right_panels: float32 [3, 65536, 2048], P(None, 'row', 'col'), may hold values from -6 to 6
- window_tiles: float32 [3, 512, 2048], P(None, 'row', 'col'), may hold values from -6 to 6
Outputs:
- updated: float32 [3, 512, 2048], P(None, 'row', 'col')
All inputs are finite; a program needn't handle non-finite values.
Results may differ from a plain program's by a relative error of at most 0.00005.
Values sent between devices are 32-bit elements; how exact they have to be, the bound alone decides.
A program may use at most 32 MiB of HBM per device.

v0:
```python
import jax
import jax.numpy as jnp
from jax import lax
from jax.sharding import PartitionSpec as P


def product(left_part, right_part):
    return jnp.dot(
        left_part, right_part, precision=lax.Precision.HIGHEST, preferred_element_type=jnp.float32
    )


def series_terms(left_parts, right_parts):
    square = product(left_parts[0], right_parts[0])
    first = product(left_parts[0], right_parts[1]) + product(left_parts[1], right_parts[0])
    second = (
        product(left_parts[0], right_parts[2])
        + product(left_parts[1], right_parts[1])
        + product(left_parts[2], right_parts[0])
    )
    return (square, first, second)


def on_device(left_panels, right_panels, window_tiles):
    width = right_panels.shape[2]
    partial_sums = jnp.concatenate(
        series_terms(lax.all_gather(left_panels, "col", axis=1, tiled=True), right_panels), axis=1
    )
    reduced = lax.psum_scatter(partial_sums, "row", scatter_dimension=0, tiled=True)
    height = reduced.shape[0]
    stacked = jnp.transpose(reduced.reshape(height, 3, width), (1, 0, 2))
    return 2.0 * window_tiles - stacked


def solution(mesh):
    return jax.shard_map(
        on_device,
        mesh=mesh,
        in_specs=(P(None, "col", "row"), P(None, "row", "col"), P(None, "row", "col")),
        out_specs=P(None, "row", "col"),
        check_vma=False,
    )
```

profile of v0, /device:TPU:1, one launch (start us, length us, event | category | flops | bytes accessed | tf_op | source)
XLA Modules:
  0.0 763.4 jit_solution(761933165146065796)
XLA Ops:
  6.5 0.0 copy-start.1
  6.5 0.0 all-gather.2.cloned.1.call-start
  6.5 0.7 all-gather.2.cloned.1.call-update
  7.3 0.0 all-reduce.3.cloned.1.call-start
  7.3 194.9 %all-gather.2.cloned.1.call-done = f32[3,512,1024]{2,1,0:T(8,128)} async-done(((f32[3,32,1024]{2,1,0:T(8,128)}), f32[3,512,1024]{2,1,0:T(8,128)}) %all-gather.2.cloned.1.call-update) | async-done | bytes 6291472 | tf_op jit(solution)/shard_map/all_gather | solution.py:27
  202.2 0.0 copy-start
  202.2 4.1 fusion
  206.3 0.0 copy-done.1
  206.4 3.9 fusion.1
  210.2 3.9 fusion.2
  214.1 0.0 copy-done
  214.1 2.3 fusion.5
  216.4 2.3 fusion.6
  218.7 2.3 fusion.8
  221.0 0.0 copy-start.2
  221.0 0.9 pad_maximum_fusion
  221.9 0.0 all-reduce.3.cloned.1.call-update
  222.0 1.3 dynamic-slice
  223.9 531.0 %all-reduce.3.cloned.1.call-done = f32[512,384]{0,1:T(8,128)} async-done(((f32[512,384]{0,1:T(8,128)}), f32[512,384]{0,1:T(8,128)}) %all-reduce.3.cloned.1.call-update) | async-done | bytes 786448
  754.9 1.0 constant_dynamic-slice_fusion
  755.9 0.1 copy.5
  756.0 0.0 copy-done.2
  756.0 0.6 bitcast_subtract_fusion
Async XLA Ops:
  6.5 199.8 %copy-start.1 = (f32[3,1024,128]{2,1,0:T(8,128)S(1)}, f32[3,1024,128]{2,1,0:T(8,128)}, u32[]{:S(2)}) copy-start(f32[3,1024,128]{2,1,0:T(8,128)} %param.4) | copy-start | bytes 4718596
  6.5 195.7 %all-gather.2.cloned.1.call-start = ((), (), s32[]{:S(2)}) async-start(), calls=%async_computation | async-start | bytes 6684672 | tf_op jit(solution)/shard_map/all_gather | solution.py:27
  7.3 747.6 %all-reduce.3.cloned.1.call-start = ((), (), s32[]{:S(2)}) async-start(), calls=%async_computation.1 | async-start | bytes 1572864
  202.2 11.9 %copy-start = (f32[3,512,1024]{2,1,0:T(8,128)S(1)}, f32[3,512,1024]{2,1,0:T(8,128)}, u32[]{:S(2)}) copy-start(f32[3,512,1024]{2,1,0:T(8,128)} %all-gather.2.cloned.1.call-done) | copy-start | bytes 18874372
  221.0 535.0 %copy-start.2 = (f32[3,8,128]{2,1,0:T(8,128)S(1)}, f32[3,8,128]{2,1,0:T(8,128)}, u32[]{:S(2)}) copy-start(f32[3,8,128]{2,1,0:T(8,128)} %param.5) | copy-start | bytes 36868
Sparse Core Ops, SparseCore 0:
  11.6 190.6 all-gather.1
  222.1 532.7 all-reduce.2
where the time goes:
time: 764 us; the launch traced here: 763 us
  waiting for transfers between devices  727 us (95%)
  matrix products  18.7 us (2%)
  between operations  14.1 us (2%)
    unnamed x3, waiting for transfers between devices  532 us
    all_gather x1, waiting for transfers between devices, on_device(): lax.all_gather(left_panels, 'col', axis=1, tiled=True)  195 us
    dot_general x6, matrix products, product(): jnp.dot(left_part, right_part, precision=lax.Precision.HIGHEST, preferred...  18.7 us
  transfers between devices with their start and end apart: 2, of which 2 were waited for; matrix products, arithmetic and copies ran while one was open for 0% of the time, Pallas kernels for 0%

commit v1 on v0

v1 whole, which is shorter than its diff:
```python
import functools

import jax
import jax.numpy as jnp
from jax import lax
from jax.experimental import pallas as pl
from jax.experimental.pallas import tpu as pltpu
from jax.sharding import PartitionSpec as P

MESH = pl.DeviceIdType.MESH
F32, BF16 = jnp.float32, jnp.bfloat16

NX, NZH, NY, NZL, NC = 4, 4, 8, 4, 2
UNITS, RU = 4, 8
SLOTS = NX * NZH

UP_ORDER = (0, 1, 2, 3)
DOWN_ORDER = (2, 3, 0, 1)


def kernel(
    l_hbm, r_hbm, w_ref, out_ref,
    gath, rv, rb, abuf, part, ybuf, zpart, zbuf,
    l_sem, r_sem, g_send, g_recv, y_send, y_recv, z_send, z_recv,
):
    depth = l_hbm.shape[2]
    cols = r_hbm.shape[2]
    row, col = lax.axis_index("row"), lax.axis_index("col")
    core = lax.rem(row, NC)
    zl = lax.rem(row // NC, NZL)
    y = row // (NC * NZL)
    x, zh = col // NZH, lax.rem(col, NZH)

    def row_of(y_, zl_, core_):
        return (y_ * NZL + zl_) * NC + core_

    def col_of(x_, zh_):
        return x_ * NZH + zh_

    steps = {
        "x+": (row, col_of(lax.rem(x + 1, NX), zh)),
        "x-": (row, col_of(lax.rem(x + NX - 1, NX), zh)),
        "z+": (row, col_of(x, lax.rem(zh + 1, NZH))),
        "z-": (row, col_of(x, lax.rem(zh + NZH - 1, NZH))),
    }
    other = lax.rem(core + 1, NC)

    barrier = pltpu.get_barrier_semaphore()
    peers = list(steps.values())
    for dy in range(NY):
        y_ = lax.rem(y + dy, NY)
        if dy:
            peers.append((row_of(y_, zl, core), col))
        peers.append((row_of(y_, zl, other), col))
    for d in range(1, NZL):
        peers.append((row_of(y, lax.rem(zl + d, NZL), core), col))
    for peer in peers:
        pl.semaphore_signal(barrier, inc=1, device_id=peer, device_id_type=MESH)

    def l_copy(s):
        return pltpu.make_async_copy(l_hbm.at[:, pl.ds(s * RU, RU), :], gath.at[0, s], l_sem.at[s])

    def r_copy(j):
        return pltpu.make_async_copy(r_hbm.at[j], rv.at[j], r_sem.at[j])

    for s in range(UNITS):
        l_copy(s).start()
    for j in range(3):
        r_copy(j).start()
    pl.semaphore_wait(barrier, len(peers))

    sent = []

    def send(step, dx, dz, s):
        if step == "x+":
            to = ((dx - 1) % NX, dz)
        elif step == "x-":
            to = ((dx + 1) % NX, dz)
        elif step == "z+":
            to = (dx, (dz - 1) % NZH)
        else:
            to = (dx, (dz + 1) % NZH)
        dst = to[0] * NZH + to[1]
        if dx == 0 and dz == 0:
            src = l_hbm.at[:, pl.ds(s * RU, RU), :]
        else:
            src = gath.at[dx * NZH + dz, s]
        copy = pltpu.make_async_remote_copy(
            src_ref=src,
            dst_ref=gath.at[dst, s],
            send_sem=g_send.at[len(sent)],
            recv_sem=g_recv.at[dst * UNITS + s],
            device_id=steps[step],
            device_id_type=MESH,
        )
        copy.start()
        sent.append(copy)

    def arrived(dx, dz, s):
        slot = dx * NZH + dz
        pltpu.make_async_remote_copy(
            src_ref=gath.at[slot, s],
            dst_ref=gath.at[slot, s],
            send_sem=g_send.at[0],
            recv_sem=g_recv.at[slot * UNITS + s],
            device_id=steps["x+"],
            device_id_type=MESH,
        ).wait_recv()

    for up, down in zip(UP_ORDER, DOWN_ORDER):
        send("z+", 0, 0, up)
        send("z-", 0, 0, down)
        send("x+", 0, 0, up)
        send("x-", 0, 0, down)

    for j in range(3):
        r_copy(j).wait()
        for k in range(0, depth, 256):
            v = rv[j, k : k + 256]
            hi = v.astype(BF16)
            rb[j, k : k + 256, :cols] = hi
            rb[j, k : k + 256, cols:] = (v - hi.astype(F32)).astype(BF16)

    def compute(slot):
        for p in range(3):
            v = gath[slot, :, p].reshape(UNITS * RU, depth)
            hi = v.astype(BF16)
            abuf[p, 0] = hi
            abuf[p, 1] = (v - hi.astype(F32)).astype(BF16)
        rows = UNITS * RU
        outs = [None] * 3
        for j in range(3):
            n = 3 - j
            prod = jnp.dot(
                abuf[:n].reshape(n * 2 * rows, depth), rb[j], preferred_element_type=F32
            )
            for p in range(n):
                hi = prod[p * 2 * rows : (p * 2 + 1) * rows]
                lo = prod[(p * 2 + 1) * rows : (p * 2 + 2) * rows]
                term = hi[:, :cols] + ((hi[:, cols:] + lo[:, :cols]) + lo[:, cols:])
                outs[p + j] = term if outs[p + j] is None else outs[p + j] + term
        for p in range(3):
            for s in range(UNITS):
                part[slot, s % NC, s // NC, p] = outs[p][s * RU : (s + 1) * RU]

    def place(slot):
        c_ = col_of(lax.rem(x + slot // NZH, NX), lax.rem(zh + slot % NZH, NZH))
        return c_ // 2, lax.rem(c_, 2)

    def y_copy(slot, j):
        y_, half = place(slot)
        core_ = lax.rem(core + j, NC)
        src = lax.rem(y - y_ + NY, NY) * NC + j
        return pltpu.make_async_remote_copy(
            src_ref=part.at[slot, core_],
            dst_ref=ybuf.at[src, half],
            send_sem=y_send.at[slot * NC + j],
            recv_sem=y_recv.at[src * 2 + half],
            device_id=(row_of(y_, zl, core_), col),
            device_id_type=MESH,
        )

    def hand_on(slot):
        y_, half = place(slot)
        y_copy(slot, 1).start()

        @pl.when(y_ != y)
        def _():
            y_copy(slot, 0).start()

        @pl.when(y_ == y)
        def _():
            ybuf[0, half] = part[slot, core]

    def block(dx, dz, units=range(UNITS)):
        for s in units:
            arrived(dx, dz, s)
        slot = dx * NZH + dz
        compute(slot)
        hand_on(slot)

    def relay(dz, units_up, units_down):
        for s in units_up:
            arrived(NX - 1, dz, s)
            send("x+", NX - 1, dz, s)
        for s in units_down:
            arrived(1, dz, s)
            send("x-", 1, dz, s)

    def spread(dz, s):
        arrived(0, dz, s)
        send("x+", 0, dz, s)
        send("x-", 0, dz, s)

    for s in range(UNITS):
        l_copy(s).wait()
    compute(0)
    hand_on(0)

    relay(0, (0,), (2,))
    relay(0, (1,), (3,))
    block(3, 0, (2, 3))
    block(1, 0, (0, 1))
    spread(3, 0), send("z+", 0, 3, 0)
    spread(1, 2), send("z-", 0, 1, 2)
    block(2, 0)
    relay(3, (0,), ())
    relay(1, (), (2,))
    spread(3, 1), send("z+", 0, 3, 1)
    spread(1, 3), send("z-", 0, 1, 3)
    relay(3, (1,), ())
    relay(1, (), (3,))
    spread(3, 2)
    spread(1, 0)
    relay(3, (), (2,))
    relay(1, (0,), ())
    spread(3, 3)
    spread(1, 1)
    relay(3, (), (3,))
    relay(1, (1,), ())
    block(0, 3, ())
    block(0, 1, ())
    block(3, 3, (2, 3))
    block(1, 3, (0, 1))
    block(3, 1, (2, 3))
    block(1, 1, (0, 1))
    spread(2, 0)
    spread(2, 2)
    block(2, 3)
    block(2, 1)
    relay(2, (0,), (2,))
    spread(2, 1)
    spread(2, 3)
    block(0, 2, ())
    relay(2, (1,), (3,))
    block(3, 2, (2, 3))
    block(1, 2, (0, 1))
    block(2, 2)

    for src in range(1, NY * NC):
        for half in range(2):
            pltpu.make_async_remote_copy(
                src_ref=ybuf.at[src, half],
                dst_ref=ybuf.at[src, half],
                send_sem=y_send.at[0],
                recv_sem=y_recv.at[src * 2 + half],
                device_id=steps["x+"],
                device_id_type=MESH,
            ).wait_recv()
    total = ybuf[0]
    for src in range(1, NY * NC):
        total = total + ybuf[src]
    zpart[...] = total.reshape(zpart.shape)

    def z_copy(d):
        zl_ = lax.rem(zl + d, NZL)
        return pltpu.make_async_remote_copy(
            src_ref=zpart.at[zl_],
            dst_ref=zbuf.at[d - 1],
            send_sem=z_send.at[d - 1],
            recv_sem=z_recv.at[d - 1],
            device_id=(row_of(y, zl_, core), col),
            device_id_type=MESH,
        )

    for d in range(1, NZL):
        z_copy(d).start()
    acc = zpart[zl]
    for d in range(1, NZL):
        z_copy(d).wait_recv()
        acc = acc + zbuf[d - 1]
    out_ref[...] = 2.0 * w_ref[...] - acc

    for copy in sent:
        copy.wait_send()
    for slot in range(SLOTS):
        y_, _ = place(slot)
        y_copy(slot, 1).wait_send()

        @pl.when(y_ != y)
        def _():
            y_copy(slot, 0).wait_send()

    for d in range(1, NZL):
        z_copy(d).wait_send()


def on_device(left_panels, right_panels, window_tiles):
    planes, height, depth = left_panels.shape
    cols = right_panels.shape[2]
    dma = pltpu.SemaphoreType.DMA
    return pl.pallas_call(
        kernel,
        out_shape=jax.ShapeDtypeStruct(window_tiles.shape, F32),
        in_specs=[
            pl.BlockSpec(memory_space=pltpu.HBM),
            pl.BlockSpec(memory_space=pltpu.HBM),
            pl.BlockSpec(memory_space=pltpu.VMEM),
        ],
        out_specs=pl.BlockSpec(memory_space=pltpu.VMEM),
        scratch_shapes=[
            pltpu.VMEM((SLOTS, UNITS, planes, RU, depth), F32),
            pltpu.VMEM((planes, depth, cols), F32),
            pltpu.VMEM((planes, depth, 2 * cols), BF16),
            pltpu.VMEM((planes, 2, height, depth), BF16),
            pltpu.VMEM((SLOTS, NC, 2, planes, RU, cols), F32),
            pltpu.VMEM((NY * NC, 2, 2, planes, RU, cols), F32),
            pltpu.VMEM((NZL, planes, RU, cols), F32),
            pltpu.VMEM((NZL - 1, planes, RU, cols), F32),
            dma((UNITS,)),
            dma((3,)),
            dma((60,)),
            dma((SLOTS * UNITS,)),
            dma((SLOTS * NC,)),
            dma((NY * NC * 2,)),
            dma((NZL - 1,)),
            dma((NZL - 1,)),
        ],
        compiler_params=pltpu.CompilerParams(
            collective_id=0, has_side_effects=True, vmem_limit_bytes=40 * 2**20
        ),
    )(left_panels, right_panels, window_tiles)


def solution(mesh):
    return jax.shard_map(
        on_device,
        mesh=mesh,
        in_specs=(P(None, "col", "row"), P(None, "row", "col"), P(None, "row", "col")),
        out_specs=P(None, "row", "col"),
        check_vma=False,
    )
```

time: 764 us -> 127 us (0.17)
  the two profiles are of different devices: /device:TPU:1 before, /device:TPU:12 now
where the time goes in v1:
time: 127 us
  Pallas kernels  123 us (97%)
  local copies, waits for them, and re-layouts  3.71 us (3%)
    pallas_call x1, Pallas kernels, on_device(): pl.pallas_call(kernel, out_shape=jax.ShapeDtypeStruct(window_tiles.shape,...  123 us
    unnamed x7, local copies, waits for them, and re-layouts  3.71 us

profile of v1, /device:TPU:12, one launch (start us, length us, event | category | flops | bytes accessed | tf_op | source)
XLA Modules:
  0.0 126.9 jit_solution(9304358745361615458)
XLA Ops:
  0.0 0.0 copy-start
  0.0 1.4 %copy-done = f32[3,1024,128]{2,1,0:T(8,128)S(1)} copy-done((f32[3,1024,128]{2,1,0:T(8,128)S(1)}, f32[3,1024,128]{2,1,0:T(8,128)}, u32[]{:S(2)}) %copy-start) | copy-done | bytes 1572888
  1.4 0.0 copy-start.1
  1.4 1.0 copy-done.1
  2.4 0.0 copy-start.2
  2.4 0.7 copy-done.2
  3.1 123.2 %shard_map.37 = f32[3,8,128]{2,1,0:T(8,128)S(1)} custom-call(f32[3,32,1024]{2,1,0:T(8,128)S(1)} %copy-done.1, f32[3,1024,128]{2,1,0:T(8,128)S(1)} %copy-done, f32[3,8,128]{2,1,0:T(8,128)S(1)} %copy-done.2), custom_call_target="tpu_custom_call" | custom-call | tf_op jit(solution)/shard_map/pallas_call | solution.py:292
  126.3 0.6 copy.5
Async XLA Ops:
  0.0 1.4 %copy-start = (f32[3,1024,128]{2,1,0:T(8,128)S(1)}, f32[3,1024,128]{2,1,0:T(8,128)}, u32[]{:S(2)}) copy-start(f32[3,1024,128]{2,1,0:T(8,128)} %r_hbm.1) | copy-start | bytes 4718596
  1.4 1.0 copy-start.1
  2.4 0.7 copy-start.2

commit v2 on v1

--- a/solution.py
+++ b/solution.py
@@ -11,17 +11,73 @@
 F32, BF16 = jnp.float32, jnp.bfloat16
 
 NX, NZH, NY, NZL, NC = 4, 4, 8, 4, 2
-UNITS, RU = 4, 8
+RU = 8
+SUB = 4
+PIECES = 2
+UNITS = SUB * PIECES
 SLOTS = NX * NZH
-
-UP_ORDER = (0, 1, 2, 3)
-DOWN_ORDER = (2, 3, 0, 1)
+UPS, DOWNS = range(UNITS // 2), range(UNITS // 2, UNITS)
+NEAR, FAR = 4, 8
+
+Z_ORDER = (
+    (0, 0), (2, 0), (0, 1), (2, 1), (0, 2), (2, 2), (0, 3), (1, 0), (2, 3), (1, 1), (0, 4), (1, 2),
+    (0, 5), (1, 3), (0, 6), (1, 4), (0, 7), (1, 5), (3, 0), (1, 6), (3, 1), (1, 7), (3, 2), (3, 3),
+)
+
+
+def z_order(step):
+    turn = 0 if step == "z+" else SUB // 2
+    return [
+        ((g + turn) % SUB * PIECES + i, h) for g, h in Z_ORDER for i in range(PIECES)
+    ]
+
+
+def plan():
+    service, lag = 2.0, 1.5 * PIECES
+    events, pending = [], []
+    done = dict.fromkeys(("x+", "x-", "z+", "z-"), 0.0)
+    ready = {(step, u, 0) for step in ("z+", "z-") for u in range(UNITS)}
+    to_send = {step: z_order(step) for step in ("z+", "z-")}
+
+    def enter(step, item, at):
+        done[step] = max(done[step], at) + service
+        pending.append((done[step] + lag, step, item))
+
+    def along_x(step, dx, dz, u, at):
+        enter(step, ((dx - 1) % NX if step == "x+" else (dx + 1) % NX, dz, u), at)
+
+    def along_z(step, at):
+        while to_send[step] and (step, *to_send[step][0]) in ready:
+            enter(step, to_send[step].pop(0), at)
+
+    along_z("z+", 0.0)
+    along_z("z-", 0.0)
+    for up, down in zip([*UPS, *DOWNS], [*DOWNS, *UPS]):
+        along_x("x+", 0, 0, up, 0.0)
+        along_x("x-", 0, 0, down, 0.0)
+    while pending:
+        pending.sort()
+        at, step, item = pending.pop(0)
+        events.append((step, *item))
+        if step in to_send:
+            u, h = item
+            ready.add((step, u, h + 1))
+            along_z(step, at)
+            if h + 1 in (NEAR, FAR):
+                dz = 2 if h + 1 == FAR else NZH - 1 if step == "z+" else 1
+                along_x("x+", 0, dz, u, at)
+                along_x("x-", 0, dz, u, at)
+        else:
+            dx, dz, u = item
+            if step == "x+" and dx == NX - 1 and u in UPS or step == "x-" and dx == 1 and u in DOWNS:
+                along_x(step, dx, dz, u, at)
+    return events
 
 
 def kernel(
     l_hbm, r_hbm, w_ref, out_ref,
-    gath, rv, rb, abuf, part, ybuf, zpart, zbuf,
-    l_sem, r_sem, g_send, g_recv, y_send, y_recv, z_send, z_recv,
+    gath, passing, rv, rb, abuf, part, ybuf, zpart, zbuf,
+    l_sem, r_sem, g_send, g_recv, p_recv, y_send, y_recv, z_send, z_recv,
 ):
     depth = l_hbm.shape[2]
     cols = r_hbm.shape[2]
@@ -40,9 +96,10 @@
     steps = {
         "x+": (row, col_of(lax.rem(x + 1, NX), zh)),
         "x-": (row, col_of(lax.rem(x + NX - 1, NX), zh)),
-        "z+": (row, col_of(x, lax.rem(zh + 1, NZH))),
-        "z-": (row, col_of(x, lax.rem(zh + NZH - 1, NZH))),
     }
+    for step, move in (("z+", 1), ("z-", NZH * NZL - 1)):
+        z_ = lax.rem(zh * NZL + zl + move, NZH * NZL)
+        steps[step] = (row_of(y, lax.rem(z_, NZL), core), col_of(x, z_ // NZL))
     other = lax.rem(core + 1, NC)
 
     barrier = pltpu.get_barrier_semaphore()
@@ -63,55 +120,71 @@
     def r_copy(j):
         return pltpu.make_async_copy(r_hbm.at[j], rv.at[j], r_sem.at[j])
 
-    for s in range(UNITS):
+    for s in range(SUB):
         l_copy(s).start()
     for j in range(3):
         r_copy(j).start()
     pl.semaphore_wait(barrier, len(peers))
 
     sent = []
-
-    def send(step, dx, dz, s):
-        if step == "x+":
-            to = ((dx - 1) % NX, dz)
-        elif step == "x-":
-            to = ((dx + 1) % NX, dz)
-        elif step == "z+":
-            to = (dx, (dz - 1) % NZH)
-        else:
-            to = (dx, (dz + 1) % NZH)
-        dst = to[0] * NZH + to[1]
-        if dx == 0 and dz == 0:
-            src = l_hbm.at[:, pl.ds(s * RU, RU), :]
-        else:
-            src = gath.at[dx * NZH + dz, s]
+    piece = depth // PIECES
+
+    def unit(slot, s):
+        return gath.at[slot, s // PIECES, :, :, pl.ds(s % PIECES * piece, piece)]
+
+    def own(s):
+        return l_hbm.at[:, pl.ds(s // PIECES * RU, RU), pl.ds(s % PIECES * piece, piece)]
+
+    def start(src, dst, recv_sem, step):
         copy = pltpu.make_async_remote_copy(
             src_ref=src,
-            dst_ref=gath.at[dst, s],
+            dst_ref=dst,
             send_sem=g_send.at[len(sent)],
-            recv_sem=g_recv.at[dst * UNITS + s],
+            recv_sem=recv_sem,
             device_id=steps[step],
             device_id_type=MESH,
         )
         copy.start()
         sent.append(copy)
 
-    def arrived(dx, dz, s):
-        slot = dx * NZH + dz
+    def wait(ref, recv_sem):
         pltpu.make_async_remote_copy(
-            src_ref=gath.at[slot, s],
-            dst_ref=gath.at[slot, s],
+            src_ref=ref,
+            dst_ref=ref,
             send_sem=g_send.at[0],
-            recv_sem=g_recv.at[slot * UNITS + s],
+            recv_sem=recv_sem,
             device_id=steps["x+"],
             device_id_type=MESH,
         ).wait_recv()
 
-    for up, down in zip(UP_ORDER, DOWN_ORDER):
-        send("z+", 0, 0, up)
-        send("z-", 0, 0, down)
-        send("x+", 0, 0, up)
-        send("x-", 0, 0, down)
+    def held(slot, s):
+        return unit(slot, s), g_recv.at[slot * UNITS + s]
+
+    def reached(step, s, h):
+        if h == NEAR:
+            return held(NZH - 1 if step == "z+" else 1, s)
+        if h == FAR:
+            return held(2, s)
+        place_ = ((0 if step == "z+" else 1) * FAR + h) * UNITS + s
+        return passing.at[place_ // PIECES, :, :, pl.ds(s % PIECES * piece, piece)], p_recv.at[place_]
+
+    to_send = {step: z_order(step) for step in ("z+", "z-")}
+    ready = {(step, u, 0) for step in to_send for u in range(UNITS)}
+
+    def send_z(step):
+        while to_send[step] and (step, *to_send[step][0]) in ready:
+            u, h = to_send[step].pop(0)
+            start(reached(step, u, h)[0] if h else own(u), *reached(step, u, h + 1), step)
+
+    def send_x(step, dx, dz, s):
+        to = (dx - 1) % NX if step == "x+" else (dx + 1) % NX
+        start(unit(dx * NZH + dz, s) if dx or dz else own(s), *held(to * NZH + dz, s), step)
+
+    send_z("z+")
+    send_z("z-")
+    for up, down in zip([*UPS, *DOWNS], [*DOWNS, *UPS]):
+        send_x("x+", 0, 0, up)
+        send_x("x-", 0, 0, down)
 
     for j in range(3):
         r_copy(j).wait()
@@ -123,11 +196,11 @@
 
     def compute(slot):
         for p in range(3):
-            v = gath[slot, :, p].reshape(UNITS * RU, depth)
+            v = gath[slot, :, p].reshape(SUB * RU, depth)
             hi = v.astype(BF16)
             abuf[p, 0] = hi
             abuf[p, 1] = (v - hi.astype(F32)).astype(BF16)
-        rows = UNITS * RU
+        rows = SUB * RU
         outs = [None] * 3
         for j in range(3):
             n = 3 - j
@@ -140,7 +213,7 @@
                 term = hi[:, :cols] + ((hi[:, cols:] + lo[:, :cols]) + lo[:, cols:])
                 outs[p + j] = term if outs[p + j] is None else outs[p + j] + term
         for p in range(3):
-            for s in range(UNITS):
+            for s in range(SUB):
                 part[slot, s % NC, s // NC, p] = outs[p][s * RU : (s + 1) * RU]
 
     def place(slot):
@@ -172,70 +245,32 @@
         def _():
             ybuf[0, half] = part[slot, core]
 
-    def block(dx, dz, units=range(UNITS)):
-        for s in units:
-            arrived(dx, dz, s)
-        slot = dx * NZH + dz
-        compute(slot)
-        hand_on(slot)
-
-    def relay(dz, units_up, units_down):
-        for s in units_up:
-            arrived(NX - 1, dz, s)
-            send("x+", NX - 1, dz, s)
-        for s in units_down:
-            arrived(1, dz, s)
-            send("x-", 1, dz, s)
-
-    def spread(dz, s):
-        arrived(0, dz, s)
-        send("x+", 0, dz, s)
-        send("x-", 0, dz, s)
-
-    for s in range(UNITS):
+    for s in range(SUB):
         l_copy(s).wait()
     compute(0)
     hand_on(0)
 
-    relay(0, (0,), (2,))
-    relay(0, (1,), (3,))
-    block(3, 0, (2, 3))
-    block(1, 0, (0, 1))
-    spread(3, 0), send("z+", 0, 3, 0)
-    spread(1, 2), send("z-", 0, 1, 2)
-    block(2, 0)
-    relay(3, (0,), ())
-    relay(1, (), (2,))
-    spread(3, 1), send("z+", 0, 3, 1)
-    spread(1, 3), send("z-", 0, 1, 3)
-    relay(3, (1,), ())
-    relay(1, (), (3,))
-    spread(3, 2)
-    spread(1, 0)
-    relay(3, (), (2,))
-    relay(1, (0,), ())
-    spread(3, 3)
-    spread(1, 1)
-    relay(3, (), (3,))
-    relay(1, (1,), ())
-    block(0, 3, ())
-    block(0, 1, ())
-    block(3, 3, (2, 3))
-    block(1, 3, (0, 1))
-    block(3, 1, (2, 3))
-    block(1, 1, (0, 1))
-    spread(2, 0)
-    spread(2, 2)
-    block(2, 3)
-    block(2, 1)
-    relay(2, (0,), (2,))
-    spread(2, 1)
-    spread(2, 3)
-    block(0, 2, ())
-    relay(2, (1,), (3,))
-    block(3, 2, (2, 3))
-    block(1, 2, (0, 1))
-    block(2, 2)
+    left = {}
+    for step, *item in plan():
+        if step in to_send:
+            u, h = item
+            wait(*reached(step, u, h + 1))
+            ready.add((step, u, h + 1))
+            send_z(step)
+            if h + 1 not in (NEAR, FAR):
+                continue
+            dx, dz = 0, 2 if h + 1 == FAR else NZH - 1 if step == "z+" else 1
+            send_x("x+", dx, dz, u)
+            send_x("x-", dx, dz, u)
+        else:
+            dx, dz, u = item
+            wait(*held(dx * NZH + dz, u))
+            if step == "x+" and dx == NX - 1 and u in UPS or step == "x-" and dx == 1 and u in DOWNS:
+                send_x(step, dx, dz, u)
+        left[dx, dz] = left.get((dx, dz), UNITS) - 1
+        if not left[dx, dz]:
+            compute(dx * NZH + dz)
+            hand_on(dx * NZH + dz)
 
     for src in range(1, NY * NC):
         for half in range(2):
@@ -299,7 +334,8 @@
         ],
         out_specs=pl.BlockSpec(memory_space=pltpu.VMEM),
         scratch_shapes=[
-            pltpu.VMEM((SLOTS, UNITS, planes, RU, depth), F32),
+            pltpu.VMEM((SLOTS, SUB, planes, RU, depth), F32),
+            pltpu.VMEM((2 * FAR * SUB, planes, RU, depth), F32),
             pltpu.VMEM((planes, depth, cols), F32),
             pltpu.VMEM((planes, depth, 2 * cols), BF16),
             pltpu.VMEM((planes, 2, height, depth), BF16),
@@ -307,17 +343,18 @@
             pltpu.VMEM((NY * NC, 2, 2, planes, RU, cols), F32),
             pltpu.VMEM((NZL, planes, RU, cols), F32),
             pltpu.VMEM((NZL - 1, planes, RU, cols), F32),
-            dma((UNITS,)),
+            dma((SUB,)),
             dma((3,)),
-            dma((60,)),
+            dma((24 * UNITS,)),
             dma((SLOTS * UNITS,)),
+            dma((2 * FAR * UNITS,)),
             dma((SLOTS * NC,)),
             dma((NY * NC * 2,)),
             dma((NZL - 1,)),
             dma((NZL - 1,)),
         ],
         compiler_params=pltpu.CompilerParams(
-            collective_id=0, has_side_effects=True, vmem_limit_bytes=40 * 2**20
+            collective_id=0, has_side_effects=True, vmem_limit_bytes=62 * 2**20
         ),
     )(left_panels, right_panels, window_tiles)
 

time: 127 us -> 105 us (0.83)
  the two profiles are of different devices: /device:TPU:12 before, /device:TPU:4 now
where the time goes in v2:
time: 105 us; the launch traced here: 104 us
  Pallas kernels  103 us (98%)
  local copies, waits for them, and re-layouts  1.31 us (1%)
    pallas_call x1, Pallas kernels, on_device(): pl.pallas_call(kernel, out_shape=jax.ShapeDtypeStruct(window_tiles.shape,...  103 us

profile of v2, /device:TPU:4, one launch (start us, length us, event | category | flops | bytes accessed | tf_op | source)
XLA Modules:
  0.0 104.3 jit_solution(14571912023949092074)
XLA Ops:
  0.0 103.0 %shard_map.37 = f32[3,8,128]{2,1,0:T(8,128)} custom-call(f32[3,32,1024]{2,1,0:T(8,128)} %l_hbm.1, f32[3,1024,128]{2,1,0:T(8,128)} %r_hbm.1, f32[3,8,128]{2,1,0:T(8,128)} %w_ref.1), custom_call_target="tpu_custom_call" | custom-call | tf_op jit(solution)/shard_map/pallas_call | solution.py:327
  103.0 1.3 %copy.5 = f32[3,8,128]{2,1,0:T(8,128)} copy(f32[3,8,128]{2,1,0:T(8,128)} %shard_map.37) | data formatting | bytes 24576

commit v3 on v2

--- a/solution.py
+++ b/solution.py
@@ -20,8 +20,8 @@
 NEAR, FAR = 4, 8
 
 Z_ORDER = (
-    (0, 0), (2, 0), (0, 1), (2, 1), (0, 2), (2, 2), (0, 3), (1, 0), (2, 3), (1, 1), (0, 4), (1, 2),
-    (0, 5), (1, 3), (0, 6), (1, 4), (0, 7), (1, 5), (3, 0), (1, 6), (3, 1), (1, 7), (3, 2), (3, 3),
+    (0, 0), (2, 0), (1, 0), (0, 1), (1, 1), (0, 2), (1, 2), (2, 1), (0, 3), (2, 2), (0, 4), (1, 3),
+    (0, 5), (2, 3), (1, 4), (0, 6), (1, 5), (0, 7), (1, 6), (3, 0), (1, 7), (3, 1), (3, 2), (3, 3),
 )
 
 
@@ -33,7 +33,7 @@
 
 
 def plan():
-    service, lag = 2.0, 1.5 * PIECES
+    service, lag = 2.0, 2.0 * PIECES
     events, pending = [], []
     done = dict.fromkeys(("x+", "x-", "z+", "z-"), 0.0)
     ready = {(step, u, 0) for step in ("z+", "z-") for u in range(UNITS)}
@@ -77,7 +77,7 @@
 def kernel(
     l_hbm, r_hbm, w_ref, out_ref,
     gath, passing, rv, rb, abuf, part, ybuf, zpart, zbuf,
-    l_sem, r_sem, g_send, g_recv, p_recv, y_send, y_recv, z_send, z_recv,
+    l_sem, r_sem, g_send, g_recv, p_recv, y_send, y_recv, z_send, z_recv, word,
 ):
     depth = l_hbm.shape[2]
     cols = r_hbm.shape[2]
@@ -103,37 +103,46 @@
     other = lax.rem(core + 1, NC)
 
     barrier = pltpu.get_barrier_semaphore()
-    peers = list(steps.values())
-    for dy in range(NY):
-        y_ = lax.rem(y + dy, NY)
-        if dy:
-            peers.append((row_of(y_, zl, core), col))
-        peers.append((row_of(y_, zl, other), col))
-    for d in range(1, NZL):
-        peers.append((row_of(y, lax.rem(zl + d, NZL), core), col))
+    for step, move in (("y+", 1), ("y-", NY - 1)):
+        steps[step] = (row_of(lax.rem(y + move, NY), zl, core), col)
+    peers = [*steps.values(), (row_of(y, zl, other), col)]
     for peer in peers:
         pl.semaphore_signal(barrier, inc=1, device_id=peer, device_id_type=MESH)
 
+    rounds = {"y+": NY // 2, "y-": NY // 2, "z+": NZL - 1, "z-": NZL - 1}
+
+    def tell(r):
+        for i, step in enumerate(rounds):
+            if r < rounds[step]:
+                pl.semaphore_signal(word.at[i], inc=1, device_id=steps[step], device_id_type=MESH)
+
+    def hear(r):
+        for i, step in enumerate(rounds):
+            if r < rounds[step]:
+                pl.semaphore_wait(word.at[i], 1)
+
+    piece = depth // PIECES
+
+    def own(s):
+        return l_hbm.at[:, pl.ds(s // PIECES * RU, RU), pl.ds(s % PIECES * piece, piece)]
+
     def l_copy(s):
-        return pltpu.make_async_copy(l_hbm.at[:, pl.ds(s * RU, RU), :], gath.at[0, s], l_sem.at[s])
+        return pltpu.make_async_copy(own(s), gath.at[0, s // PIECES, s % PIECES], l_sem.at[s])
 
     def r_copy(j):
         return pltpu.make_async_copy(r_hbm.at[j], rv.at[j], r_sem.at[j])
 
-    for s in range(SUB):
+    for s in range(UNITS):
         l_copy(s).start()
     for j in range(3):
         r_copy(j).start()
     pl.semaphore_wait(barrier, len(peers))
+    tell(0)
 
     sent = []
-    piece = depth // PIECES
 
     def unit(slot, s):
-        return gath.at[slot, s // PIECES, :, :, pl.ds(s % PIECES * piece, piece)]
-
-    def own(s):
-        return l_hbm.at[:, pl.ds(s // PIECES * RU, RU), pl.ds(s % PIECES * piece, piece)]
+        return gath.at[slot, s // PIECES, s % PIECES]
 
     def start(src, dst, recv_sem, step):
         copy = pltpu.make_async_remote_copy(
@@ -166,7 +175,7 @@
         if h == FAR:
             return held(2, s)
         place_ = ((0 if step == "z+" else 1) * FAR + h) * UNITS + s
-        return passing.at[place_ // PIECES, :, :, pl.ds(s % PIECES * piece, piece)], p_recv.at[place_]
+        return passing.at[place_], p_recv.at[place_]
 
     to_send = {step: z_order(step) for step in ("z+", "z-")}
     ready = {(step, u, 0) for step in to_send for u in range(UNITS)}
@@ -194,13 +203,15 @@
             rb[j, k : k + 256, :cols] = hi
             rb[j, k : k + 256, cols:] = (v - hi.astype(F32)).astype(BF16)
 
-    def compute(slot):
+    def compute(slot, h):
         for p in range(3):
-            v = gath[slot, :, p].reshape(SUB * RU, depth)
-            hi = v.astype(BF16)
-            abuf[p, 0] = hi
-            abuf[p, 1] = (v - hi.astype(F32)).astype(BF16)
-        rows = SUB * RU
+            for i in range(PIECES):
+                v = gath[slot, h * NC : (h + 1) * NC, i, p].reshape(NC * RU, piece)
+                hi = v.astype(BF16)
+                ks = slice(i * piece, (i + 1) * piece)
+                abuf[p, 0, :, ks] = hi
+                abuf[p, 1, :, ks] = (v - hi.astype(F32)).astype(BF16)
+        rows = NC * RU
         outs = [None] * 3
         for j in range(3):
             n = 3 - j
@@ -213,45 +224,49 @@
                 term = hi[:, :cols] + ((hi[:, cols:] + lo[:, :cols]) + lo[:, cols:])
                 outs[p + j] = term if outs[p + j] is None else outs[p + j] + term
         for p in range(3):
-            for s in range(SUB):
-                part[slot, s % NC, s // NC, p] = outs[p][s * RU : (s + 1) * RU]
+            for s in range(NC):
+                part[slot, s, h, p] = outs[p][s * RU : (s + 1) * RU]
 
     def place(slot):
         c_ = col_of(lax.rem(x + slot // NZH, NX), lax.rem(zh + slot % NZH, NZH))
         return c_ // 2, lax.rem(c_, 2)
 
-    def y_copy(slot, j):
+    def y_copy(slot, j, h):
         y_, half = place(slot)
         core_ = lax.rem(core + j, NC)
         src = lax.rem(y - y_ + NY, NY) * NC + j
         return pltpu.make_async_remote_copy(
-            src_ref=part.at[slot, core_],
-            dst_ref=ybuf.at[src, half],
-            send_sem=y_send.at[slot * NC + j],
-            recv_sem=y_recv.at[src * 2 + half],
+            src_ref=part.at[slot, core_, h],
+            dst_ref=ybuf.at[src, half, h],
+            send_sem=y_send.at[(slot * NC + j) * 2 + h],
+            recv_sem=y_recv.at[(src * 2 + half) * 2 + h],
             device_id=(row_of(y_, zl, core_), col),
             device_id_type=MESH,
         )
 
-    def hand_on(slot):
+    def hand_on(slot, h):
         y_, half = place(slot)
-        y_copy(slot, 1).start()
+        y_copy(slot, 1, h).start()
 
         @pl.when(y_ != y)
         def _():
-            y_copy(slot, 0).start()
+            y_copy(slot, 0, h).start()
 
         @pl.when(y_ == y)
         def _():
-            ybuf[0, half] = part[slot, core]
-
-    for s in range(SUB):
+            ybuf[0, half, h] = part[slot, core, h]
+
+    for s in range(UNITS):
         l_copy(s).wait()
-    compute(0)
-    hand_on(0)
+    ended = [(0, 0), (0, 1)]
+    for slot, h in ended:
+        compute(slot, h)
 
     left = {}
-    for step, *item in plan():
+    for count, (step, *item) in enumerate(plan()):
+        if count % 6 == 5 and count // 6 < NY // 2:
+            hear(count // 6)
+            tell(count // 6 + 1)
         if step in to_send:
             u, h = item
             wait(*reached(step, u, h + 1))
@@ -267,21 +282,18 @@
             wait(*held(dx * NZH + dz, u))
             if step == "x+" and dx == NX - 1 and u in UPS or step == "x-" and dx == 1 and u in DOWNS:
                 send_x(step, dx, dz, u)
-        left[dx, dz] = left.get((dx, dz), UNITS) - 1
-        if not left[dx, dz]:
-            compute(dx * NZH + dz)
-            hand_on(dx * NZH + dz)
+        h = u // (UNITS // 2)
+        left[dx, dz, h] = left.get((dx, dz, h), UNITS // 2) - 1
+        if not left[dx, dz, h]:
+            compute(dx * NZH + dz, h)
+            ended.append((dx * NZH + dz, h))
+        if count >= 6 * (NY // 2):
+            while ended:
+                hand_on(*ended.pop(0))
 
     for src in range(1, NY * NC):
-        for half in range(2):
-            pltpu.make_async_remote_copy(
-                src_ref=ybuf.at[src, half],
-                dst_ref=ybuf.at[src, half],
-                send_sem=y_send.at[0],
-                recv_sem=y_recv.at[src * 2 + half],
-                device_id=steps["x+"],
-                device_id_type=MESH,
-            ).wait_recv()
+        for i in range(4):
+            wait(ybuf.at[src, i // 2, i % 2], y_recv.at[src * 4 + i])
     total = ybuf[0]
     for src in range(1, NY * NC):
         total = total + ybuf[src]
@@ -310,11 +322,13 @@
         copy.wait_send()
     for slot in range(SLOTS):
         y_, _ = place(slot)
-        y_copy(slot, 1).wait_send()
+        for h in range(2):
+            y_copy(slot, 1, h).wait_send()
 
         @pl.when(y_ != y)
         def _():
-            y_copy(slot, 0).wait_send()
+            for h in range(2):
+                y_copy(slot, 0, h).wait_send()
 
     for d in range(1, NZL):
         z_copy(d).wait_send()
@@ -334,24 +348,25 @@
         ],
         out_specs=pl.BlockSpec(memory_space=pltpu.VMEM),
         scratch_shapes=[
-            pltpu.VMEM((SLOTS, SUB, planes, RU, depth), F32),
-            pltpu.VMEM((2 * FAR * SUB, planes, RU, depth), F32),
+            pltpu.VMEM((SLOTS, SUB, PIECES, planes, RU, depth // PIECES), F32),
+            pltpu.VMEM((2 * FAR * UNITS, planes, RU, depth // PIECES), F32),
             pltpu.VMEM((planes, depth, cols), F32),
             pltpu.VMEM((planes, depth, 2 * cols), BF16),
-            pltpu.VMEM((planes, 2, height, depth), BF16),
+            pltpu.VMEM((planes, 2, NC * RU, depth), BF16),
             pltpu.VMEM((SLOTS, NC, 2, planes, RU, cols), F32),
             pltpu.VMEM((NY * NC, 2, 2, planes, RU, cols), F32),
             pltpu.VMEM((NZL, planes, RU, cols), F32),
             pltpu.VMEM((NZL - 1, planes, RU, cols), F32),
-            dma((SUB,)),
+            dma((UNITS,)),
             dma((3,)),
             dma((24 * UNITS,)),
             dma((SLOTS * UNITS,)),
             dma((2 * FAR * UNITS,)),
-            dma((SLOTS * NC,)),
-            dma((NY * NC * 2,)),
+            dma((SLOTS * NC * 2,)),
+            dma((NY * NC * 4,)),
             dma((NZL - 1,)),
             dma((NZL - 1,)),
+            pltpu.SemaphoreType.REGULAR((4,)),
         ],
         compiler_params=pltpu.CompilerParams(
             collective_id=0, has_side_effects=True, vmem_limit_bytes=62 * 2**20

time: 105 us -> 103 us (0.981)
  Pallas kernels: 103 us -> 101 us
    pallas_call x1, Pallas kernels: 103 us -> 101 us  [on_device(): pl.pallas_call(kernel, out_shape=jax.ShapeDtypeStruct(window_tiles.shape,...]
where the time goes in v3:
time: 103 us; the launch traced here: 102 us
  Pallas kernels  101 us (98%)
  local copies, waits for them, and re-layouts  1.31 us (1%)
    pallas_call x1, Pallas kernels, on_device(): pl.pallas_call(kernel, out_shape=jax.ShapeDtypeStruct(window_tiles.shape,...  101 us

profile of v3, /device:TPU:4, one launch (start us, length us, event | category | flops | bytes accessed | tf_op | source)
XLA Modules:
  0.0 102.5 jit_solution(340788393921391697)
XLA Ops:
  0.0 101.2 %shard_map.37 = f32[3,8,128]{2,1,0:T(8,128)} custom-call(f32[3,32,1024]{2,1,0:T(8,128)} %l_hbm.1, f32[3,1024,128]{2,1,0:T(8,128)} %r_hbm.1, f32[3,8,128]{2,1,0:T(8,128)} %w_ref.1), custom_call_target="tpu_custom_call" | custom-call | tf_op jit(solution)/shard_map/pallas_call | solution.py:341
  101.2 1.3 %copy.5 = f32[3,8,128]{2,1,0:T(8,128)} copy(f32[3,8,128]{2,1,0:T(8,128)} %shard_map.37) | data formatting | bytes 24576
